TPU v7x, 32 devices: a whole 2x2x4 slice. The times are simulated.
32 devices in a mesh: island: 8 (over y, x, core), fsdp: 4 (over z).
Axes of the slice: x: 2, y: 2, z: 4, core: 2. Of those that a mesh axis runs over, the one named last changes fastest.
Arguments:
- tokens: bfloat16 [8, 1024, 8192], P('island', 'fsdp'), may hold values from -6 to 6
- cotangent: bfloat16 [8, 1024, 1024], P('island', 'fsdp'), may hold values from -0.1875 to 0.1875
- params: float32 [8, 8192, 1024], P('island', 'fsdp'), may hold values from -0.18 to 0.18
- first_moment: bfloat16 [8, 8192, 1024], P('island', 'fsdp'), may hold values from -3 to 3
- second_moment: bfloat16 [8, 8192, 1024], P('island', 'fsdp'), may hold values from 0.25 to 4
- base: float32 [8192, 512], P(('fsdp', 'island')), may hold values from -0.18 to 0.18
- outer_momentum: float32 [8192, 512], P(('fsdp', 'island')), may hold values from -0.06 to 0.06
- head_order: int32 [8], replicated, may hold values from 0 to 7, each once
- step_fragment: int32 [1], replicated, may hold values from 0 to 1
Outputs:
- params_out: float32 [8, 8192, 1024], P('island', 'fsdp')
- first_out: bfloat16 [8, 8192, 1024], P('island', 'fsdp')
- second_out: bfloat16 [8, 8192, 1024], P('island', 'fsdp')
- base_out: float32 [8192, 512], P(('fsdp', 'island'))
- momentum_out: float32 [8192, 512], P(('fsdp', 'island'))
All inputs are finite; a program needn't handle non-finite values.
Results may differ from a plain program's by a relative error of at most 0.012.
Values may be sent and summed in bfloat16 or wider, within the bound.
No kernel may reach another device: no remote copies, remote signals or barrier semaphores. Data moves between devices by JAX's collectives and lax.ppermute only.
A program may use at most 128 MiB of HBM per device.

v0:
```python
import jax
import jax.numpy as jnp
from jax import lax
from jax.sharding import PartitionSpec as P

KVH = 8
HD = 128
SYNC = 4


def outer_update(base, outer_momentum, total, islands):
    delta = base - total / islands
    momentum = 0.9 * outer_momentum + delta
    return (base - 0.7 * (delta + 0.9 * momentum), momentum)


def shards(
    tokens,
    cotangent,
    params,
    first_moment,
    second_moment,
    base,
    outer_momentum,
    head_order,
    step_fragment,
):
    local_tokens = tokens[0]
    weights = params[0]
    rows = weights.shape[0]
    width = weights.shape[1]
    block = local_tokens.shape[0]
    columns = lax.all_to_all(tokens, "fsdp", split_axis=2, concat_axis=1, tiled=True)[0]
    piece = lax.all_gather(cotangent, "fsdp", axis=1, tiled=True)
    blocks = piece.shape[1] // block

    def one_block(index, running):
        grads_part = lax.dynamic_slice_in_dim(piece[0], index * block, block, 0)
        token_part = lax.dynamic_slice_in_dim(columns, index * block, block, 0)
        part = lax.dot_general(
            token_part, grads_part, (((0,), (0,)), ((), ())), preferred_element_type=jnp.float32
        )
        part = lax.optimization_barrier(part.astype(jnp.bfloat16)).astype(jnp.float32)
        return running + part

    grad = lax.fori_loop(0, blocks, one_block, jnp.zeros((rows, width), jnp.float32))
    moment_one = 0.9 * first_moment[0].astype(jnp.float32) + 0.1 * grad
    moment_two = 0.95 * second_moment[0].astype(jnp.float32) + 0.05 * grad * grad
    stepped = weights - 0.01 * (moment_one / (jnp.sqrt(moment_two) + 1e-08) + 0.1 * weights)
    heads = lax.dynamic_slice(head_order, (step_fragment[0] * SYNC,), (SYNC,))
    shaped = stepped.reshape(rows, KVH, HD)
    fragment = jnp.take(shaped, heads, axis=1).reshape(rows, SYNC * HD)
    islands = lax.axis_size("island")
    total = lax.psum_scatter(
        fragment.astype(jnp.bfloat16), "island", scatter_dimension=0, tiled=True
    ).astype(jnp.float32)
    base_next, momentum_next = outer_update(base, outer_momentum, total, islands)
    whole_base = lax.all_gather(
        base_next.astype(jnp.bfloat16), "island", axis=0, tiled=True
    ).astype(base_next.dtype)
    updated = shaped.at[:, heads, :].set(whole_base.reshape(rows, SYNC, HD)).reshape(rows, width)
    return (
        updated[None],
        moment_one.astype(jnp.bfloat16)[None],
        moment_two.astype(jnp.bfloat16)[None],
        base_next,
        momentum_next,
    )


def solution(mesh):
    placed = (
        P("island", "fsdp", None),
        P("island", "fsdp", None),
        P("island", "fsdp", None),
        P("island", "fsdp", None),
        P("island", "fsdp", None),
        P(("fsdp", "island"), None),
        P(("fsdp", "island"), None),
        P(),
        P(),
    )
    return jax.shard_map(
        shards,
        mesh=mesh,
        in_specs=placed,
        out_specs=(
            P("island", "fsdp", None),
            P("island", "fsdp", None),
            P("island", "fsdp", None),
            P(("fsdp", "island"), None),
            P(("fsdp", "island"), None),
        ),
        check_vma=False,
    )
```

profile of v0, /device:TPU:0, one launch (start us, length us, event | category | flops | bytes accessed | tf_op | source)
XLA Modules:
  0.0 422.3 jit_solution(16253507385062909303)
XLA Ops:
  7.2 17.8 %copy.73 = bf16[1,256,8192]{1,0,2:T(2,128)(2,1)} copy(bf16[1,256,8192]{2,1,0:T(8,128)(2,1)} %param.11) | data formatting | bytes 8388608 | tf_op args[0]
  25.4 43.5 %reduce = bf16[8192,256]{1,0:T(8,128)(2,1)} reduce(bf16[8192,1,256]{2,1,0:T(2,128)(2,1)} %bitcast.56, bf16[]{:T(256)} %broadcast.57), dimensions={1}, to_apply=%bitcast.50.reduce_sub_computation | reduce | bytes 8388610
  74.1 6.3 %all-to-all-start = ((bf16[4,2,262144]{2,1,0:T(2,128)(2,1)}), bf16[4,2,262144]{2,1,0:T(2,128)(2,1)}, u32[]{:S(2)}, u32[]{:S(2)}) async-start(bf16[4,2,262144]{2,1,0:T(2,128)(2,1)} %reshape.62), calls=%async_computation | async-start | bytes 8388608 | tf_op jit(solution)/shard_map/all_to_all | solution.py:33
  82.0 9.3 %copy.71 = f32[1,2048,1024]{1,2,0:T(8,128)} copy(f32[1,2048,1024]{2,1,0:T(8,128)} %param.13) | data formatting | bytes 16777216 | tf_op args[2]
  91.3 6.6 %copy.72 = bf16[1,2048,1024]{1,2,0:T(8,128)(2,1)} copy(bf16[1,2048,1024]{2,1,0:T(8,128)(2,1)} %param.14) | data formatting | bytes 8388608 | tf_op args[3]
  97.9 6.5 %copy.76 = bf16[1,2048,1024]{1,2,0:T(8,128)(2,1)} copy(bf16[1,2048,1024]{2,1,0:T(8,128)(2,1)} %param.15) | data formatting | bytes 8388608 | tf_op args[4]
  104.6 103.0 %all-to-all-done = bf16[4,2,262144]{2,1,0:T(2,128)(2,1)} async-done(((bf16[4,2,262144]{2,1,0:T(2,128)(2,1)}), bf16[4,2,262144]{2,1,0:T(2,128)(2,1)}, u32[]{:S(2)}, u32[]{:S(2)}) %all-to-all-start) | async-done | bytes 4194336 | tf_op jit(solution)/shard_map/all_to_all | solution.py:33
  207.6 7.4 %reshape.63 = bf16[8192,1,256]{2,1,0:T(2,128)(2,1)} reshape(bf16[4,2,262144]{2,1,0:T(2,128)(2,1)} %all-to-all-done) | data formatting | bytes 8388608
  215.0 6.1 %copy.90 = bf16[1,256,8192]{1,2,0:T(8,128)(2,1)} copy(bf16[1,256,8192]{1,0,2:T(2,128)(2,1)} %bitcast.57) | data formatting | bytes 8388608
  221.1 6.2 %copy.74 = bf16[1,4,256,2048]{3,2,1,0:T(8,128)(2,1)} copy(bf16[1,4,256,2048]{2,3,1,0:T(8,128)(2,1)} %bitcast.60) | data formatting | bytes 8388608 | tf_op jit(solution)/shard_map/all_to_all | solution.py:33
  227.3 57.0 %while.14 = (s32[]{:T(128)}, f32[2048,1024]{1,0:T(8,128)}, bf16[1024,2048]{1,0:T(8,128)(2,1)}, bf16[1,1024,1024]{2,1,0:T(8,128)(2,1)}, s32[]{:T(128)}, /*index=5*/s32[]{:T(128)}, s32[]{:T(128)}, s32[]{:T(128)}) while((s32[]{:T(128)}, f32[2048,1024]{1,0:T(8,128)}, bf16[1024,2048]{1,0:T(8,128)(2,1)}, ...), condition=%wide.region_1.0_spmd.clone, body=%wide.region_0.0_spmd.clone.sunk | while | flops 1082130432 | bytes 26739852 | solution.py:46
  231.9 7.8 %select_add_fusion.2 = f32[2048,1024]{1,0:T(8,128)} fusion(f32[2048,1024]{1,0:T(8,128)} %get-tuple-element.170, bf16[2048,1024]{1,0:T(8,128)(2,1)} %convolution_convert_fusion.2, pred[]{:T(512)S(6)} %compare.3), kind=kLoop, calls=%fused_computation.2.clone.1 | loop fusion | flops 6291456 | bytes 20971520 | tf_op jit(solution)/shard_map/while/body/eval_jaxpr/add | solution.py:44
  244.4 10.2 %select_add_fusion.2 = f32[2048,1024]{1,0:T(8,128)} fusion(f32[2048,1024]{1,0:T(8,128)} %get-tuple-element.170, bf16[2048,1024]{1,0:T(8,128)(2,1)} %convolution_convert_fusion.2, pred[]{:T(512)S(6)} %compare.3), kind=kLoop, calls=%fused_computation.2.clone.1 | loop fusion | flops 6291456 | bytes 20971520 | tf_op jit(solution)/shard_map/while/body/eval_jaxpr/add | solution.py:44
  259.3 10.2 %select_add_fusion.2 = f32[2048,1024]{1,0:T(8,128)} fusion(f32[2048,1024]{1,0:T(8,128)} %get-tuple-element.170, bf16[2048,1024]{1,0:T(8,128)(2,1)} %convolution_convert_fusion.2, pred[]{:T(512)S(6)} %compare.3), kind=kLoop, calls=%fused_computation.2.clone.1 | loop fusion | flops 6291456 | bytes 20971520 | tf_op jit(solution)/shard_map/while/body/eval_jaxpr/add | solution.py:44
  274.1 10.2 %select_add_fusion.2 = f32[2048,1024]{1,0:T(8,128)} fusion(f32[2048,1024]{1,0:T(8,128)} %get-tuple-element.170, bf16[2048,1024]{1,0:T(8,128)(2,1)} %convolution_convert_fusion.2, pred[]{:T(512)S(6)} %compare.3), kind=kLoop, calls=%fused_computation.2.clone.1 | loop fusion | flops 6291456 | bytes 20971520 | tf_op jit(solution)/shard_map/while/body/eval_jaxpr/add | solution.py:44
  284.3 9.2 %copy.75 = f32[2048,1024]{0,1:T(8,128)} copy(f32[2048,1024]{1,0:T(8,128)} %get-tuple-element.84) | data formatting | bytes 16777216 | tf_op jit(solution)/shard_map/while | solution.py:46
  293.5 15.2 %fusion.9 = (bf16[1,2048,1024]{1,2,0:T(8,128)(2,1)}, f32[2048,1024]{0,1:T(8,128)}, bf16[1,2048,1024]{1,2,0:T(8,128)(2,1)}) fusion(f32[2048,1024]{0,1:T(8,128)} %copy.75, bf16[1,2048,1024]{1,2,0:T(8,128)(2,1)} %copy.76, bf16[1,2048,1024]{1,2,0:T(8,128)(2,1)} %copy.72, f32[1,2048,1024]{1,2,0:T(8,128)} %copy.71), kind=kLoop, calls=%fused_computation.17 | loop fusion | flops 35651584 | bytes 41943040 | tf_op jit(solution)/shard_map/broadcast_in_dim | solution.py:65
  315.4 39.6 %reduce-scatter.2.cloned.1.call-done = bf16[256,512]{0,1:T(8,128)(2,1)} async-done(((bf16[2048,512]{0,1:T(8,128)(2,1)}), bf16[256,512]{0,1:T(8,128)(2,1)}) %reduce-scatter.2.cloned.1.call-update) | async-done | bytes 262160 | tf_op jit(solution)/shard_map/reduce_scatter | solution.py:54
  356.9 9.2 %copy.83 = f32[2048,8,128]{2,0,1:T(8,128)} copy(f32[2048,8,128]{0,2,1:T(8,128)} %bitcast.55) | data formatting | bytes 16777216 | tf_op jit(solution)/shard_map/reshape | solution.py:51
  366.1 6.4 %copy.86 = bf16[1,2048,1024]{2,1,0:T(8,128)(2,1)} copy(bf16[1,2048,1024]{1,2,0:T(8,128)(2,1)} %get-tuple-element.134) | data formatting | bytes 8388608
  372.5 6.3 %copy.87 = bf16[1,2048,1024]{2,1,0:T(8,128)(2,1)} copy(bf16[1,2048,1024]{1,2,0:T(8,128)(2,1)} %get-tuple-element.132) | data formatting | bytes 8388608
  389.3 8.1 %scatter_fusion = f32[2048,8,128]{2,0,1:T(8,128)} fusion(f32[2048,8,128]{2,0,1:T(8,128)} %copy.83, s32[4]{0:T(128)S(1)} %get-tuple-element.131, f32[4,2048,128]{2,1,0:T(8,128)} %bitcast.61), kind=kCustom, calls=%fused_computation.1 | custom fusion | bytes 12582928 | tf_op jit(solution)/shard_map/scatter | solution.py:61
  397.3 9.2 %copy.84 = f32[2048,8,128]{0,2,1:T(8,128)} copy(f32[2048,8,128]{2,0,1:T(8,128)} %scatter_fusion) | data formatting | bytes 16777216 | tf_op jit(solution)/shard_map/scatter | solution.py:61
  406.6 9.2 %copy.85 = f32[1,2048,1024]{2,1,0:T(8,128)} copy(f32[1,2048,1024]{1,2,0:T(8,128)} %bitcast.58) | data formatting | bytes 16777216
  (32 shorter events, 44.3 us)
Async XLA Ops:
  74.1 133.5 %all-to-all-start = ((bf16[4,2,262144]{2,1,0:T(2,128)(2,1)}), bf16[4,2,262144]{2,1,0:T(2,128)(2,1)}, u32[]{:S(2)}, u32[]{:S(2)}) async-start(bf16[4,2,262144]{2,1,0:T(2,128)(2,1)} %reshape.62), calls=%async_computation | async-start | bytes 8388608 | tf_op jit(solution)/shard_map/all_to_all | solution.py:33
  80.4 146.9 %all-gather.3.cloned.1.call-start = ((), (), s32[]{:S(2)}) async-start(), calls=%async_computation.2 | async-start | bytes 2621440 | tf_op jit(solution)/shard_map/all_gather | solution.py:34
  81.1 273.9 %reduce-scatter.2.cloned.1.call-start = ((), (), s32[]{:S(2)}) async-start(), calls=%async_computation.3 | async-start | bytes 2359296 | tf_op jit(solution)/shard_map/reduce_scatter | solution.py:54
  91.3 13.1 %copy-start.2 = (s32[8]{0:T(128)S(1)}, s32[8]{0:T(128)}, u32[]{:S(2)}) copy-start(s32[8]{0:T(128)} %param.18) | copy-start | bytes 100
  308.7 6.3 %copy-start = (f32[256,512]{1,0:T(8,128)S(1)}, f32[256,512]{1,0:T(8,128)}, u32[]{:S(2)}) copy-start(f32[256,512]{1,0:T(8,128)} %param.17) | copy-start | bytes 1572868
  308.7 6.5 %copy-start.1 = (f32[256,512]{1,0:T(8,128)S(1)}, f32[256,512]{1,0:T(8,128)}, u32[]{:S(2)}) copy-start(f32[256,512]{1,0:T(8,128)} %param.16) | copy-start | bytes 1572868
  314.7 70.4 %all-gather.5.cloned.1.call-start = ((), (), s32[]{:S(2)}) async-start(), calls=%async_computation.4 | async-start | bytes 2359296 | tf_op jit(solution)/shard_map/all_gather | solution.py:58
Sparse Core Ops, SparseCore 0:
  82.8 77.2 all-gather.2
  314.9 40.1 reduce-scatter.1
  357.1 28.0 all-gather.4
where the time goes:
time: 425 us; the launch traced here: 422 us
  waiting for transfers between devices  148 us (35%)
  local copies, waits for them, and re-layouts  134 us (32%)
  other arithmetic  101 us (24%)
  matrix products  18.6 us (4%)
  between operations  14.5 us (3%)
  starting transfers between devices  6.83 us (2%)
    all_to_all x1, waiting for transfers between devices, shards(): lax.all_to_all(tokens, 'fsdp', split_axis=2, concat_axis=1, tiled=True)[0]  103 us
    unnamed x21, local copies, waits for them, and re-layouts  83.5 us
    unnamed x2, other arithmetic  43.5 us
    reduce_scatter x1, waiting for transfers between devices, shards(): lax.psum_scatter(fragment.astype(jnp.bfloat16), 'island', scatter_dimensi...  39.6 us
    add x4, other arithmetic, one_block(): return running + part  38.4 us
    dot_general x4, matrix products, one_block(): lax.dot_general(token_part, grads_part, (((0,), (0,)), ((), ())), preferr...  18.6 us
    scatter x2, local copies, waits for them, and re-layouts, shards(): shaped.at[:, heads, :].set(whole_base.reshape(rows, SYNC, HD))  17.3 us
    broadcast_in_dim x1, other arithmetic, shards(): moment_two.astype(jnp.bfloat16)[None]  15.2 us
  transfers between devices with their start and end apart: 4, of which 3 were waited for; matrix products, arithmetic and copies ran while one was open for 16% of the time, Pallas kernels for 0%

commit v1 on v0

--- a/solution.py
+++ b/solution.py
@@ -6,6 +6,29 @@
 KVH = 8
 HD = 128
 SYNC = 4
+
+
+def cut_along(x, dim, count):
+    shape = x.shape
+    pieces = x.reshape(*shape[:dim], count, shape[dim] // count, *shape[dim + 1 :])
+    return jnp.moveaxis(pieces, dim, 0)
+
+
+def joined_along(pieces, dim):
+    dims = list(pieces.shape[1:])
+    dims[dim] *= pieces.shape[0]
+    return jnp.moveaxis(pieces, 0, dim).reshape(dims)
+
+
+def sent_to_each(x, axis, split_dim, concat_dim):
+    count, here = (lax.axis_size(axis), lax.axis_index(axis))
+    blocks = cut_along(x, split_dim, count)
+    finished = [blocks[here]]
+    for turn in range(1, count):
+        sent = blocks[(here + turn) % count]
+        finished.append(lax.ppermute(sent, axis, [(i, (i + turn) % count) for i in range(count)]))
+    blocks = jnp.stack(finished)[(here - jnp.arange(count)) % count]
+    return joined_along(blocks, concat_dim)
 
 
 def outer_update(base, outer_momentum, total, islands):
@@ -30,7 +53,7 @@
     rows = weights.shape[0]
     width = weights.shape[1]
     block = local_tokens.shape[0]
-    columns = lax.all_to_all(tokens, "fsdp", split_axis=2, concat_axis=1, tiled=True)[0]
+    columns = sent_to_each(tokens, "fsdp", 2, 1)[0]
     piece = lax.all_gather(cotangent, "fsdp", axis=1, tiled=True)
     blocks = piece.shape[1] // block
 

time: 425 us -> 352 us (0.83)
  other arithmetic: 101 us -> 60.9 us
  local copies, waits for them, and re-layouts: 134 us -> 110 us
  waiting for transfers between devices: 148 us -> 139 us
    all_to_all x1 -> x0, waiting for transfers between devices: 103 us -> none  [shards(): lax.all_to_all(tokens, 'fsdp', split_axis=2, concat_axis=1, tiled=True)[0]]
    ppermute x0 -> x3, waiting for transfers between devices: none -> 72.2 us  [sent_to_each(): lax.ppermute(sent, axis, [(i, (i + turn) % count) for i in range(count)])]
    unnamed x2 -> x1, other arithmetic: 43.5 us -> 0.01 us
    unnamed x21 -> x17, local copies, waits for them, and re-layouts: 83.5 us -> 53 us
    reduce_scatter x1, waiting for transfers between devices: 39.6 us -> 61.7 us  [shards(): lax.psum_scatter(fragment.astype(jnp.bfloat16), 'island', scatter_dimensi...]
    another operation x0 -> x5, local copies, waits for them, and re-layouts: none -> 8.42 us
    ppermute x0 -> x3, starting transfers between devices: none -> 7.05 us  [sent_to_each(): lax.ppermute(sent, axis, [(i, (i + turn) % count) for i in range(count)])]
    all_to_all x1 -> x0, starting transfers between devices: 6.35 us -> none  [shards(): lax.all_to_all(tokens, 'fsdp', split_axis=2, concat_axis=1, tiled=True)[0]]
  transfers between devices with their start and end apart: 4 -> 6, of which waited for: 3 -> 4; matrix products, arithmetic and copies ran while one was open for 16% -> 20% of each run, Pallas kernels for 0% -> 0%
where the time goes in v1:
time: 352 us; the launch traced here: 351 us
  waiting for transfers between devices  139 us (39%)
  local copies, waits for them, and re-layouts  110 us (31%)
  other arithmetic  60.9 us (17%)
  matrix products  18.6 us (5%)
  between operations  14.6 us (4%)
  starting transfers between devices  7.35 us (2%)
    ppermute x3, waiting for transfers between devices, sent_to_each(): lax.ppermute(sent, axis, [(i, (i + turn) % count) for i in range(count)])  72.2 us
    reduce_scatter x1, waiting for transfers between devices, shards(): lax.psum_scatter(fragment.astype(jnp.bfloat16), 'island', scatter_dimensi...  61.7 us
    unnamed x17, local copies, waits for them, and re-layouts  53 us
    add x4, other arithmetic, one_block(): return running + part  38.4 us
    dot_general x4, matrix products, one_block(): lax.dot_general(token_part, grads_part, (((0,), (0,)), ((), ())), preferr...  18.6 us
    scatter x2, local copies, waits for them, and re-layouts, shards(): shaped.at[:, heads, :].set(whole_base.reshape(rows, SYNC, HD))  17.2 us
    broadcast_in_dim x1, other arithmetic, shards(): moment_two.astype(jnp.bfloat16)[None]  15.2 us
    reshape x1, local copies, waits for them, and re-layouts, shards(): shaped = stepped.reshape(rows, KVH, HD)  9.2 us
  transfers between devices with their start and end apart: 6, of which 4 were waited for; matrix products, arithmetic and copies ran while one was open for 20% of the time, Pallas kernels for 0%

profile of v1, /device:TPU:0, one launch (start us, length us, event | category | flops | bytes accessed | tf_op | source)
XLA Modules:
  0.0 350.7 jit_solution(18204405647031848793)
XLA Ops:
  8.0 6.4 %copy.34 = bf16[1,256,8192]{1,2,0:T(8,128)(2,1)} copy(bf16[1,256,8192]{2,1,0:T(8,128)(2,1)} %param.11) | data formatting | bytes 8388608 | tf_op args[0]
  29.9 9.2 %copy.32 = f32[1,2048,1024]{1,2,0:T(8,128)} copy(f32[1,2048,1024]{2,1,0:T(8,128)} %param.13) | data formatting | bytes 16777216 | tf_op args[2]
  39.1 6.5 %copy.33 = bf16[1,2048,1024]{1,2,0:T(8,128)(2,1)} copy(bf16[1,2048,1024]{2,1,0:T(8,128)(2,1)} %param.14) | data formatting | bytes 8388608 | tf_op args[3]
  45.6 6.6 %copy.40 = bf16[1,2048,1024]{1,2,0:T(8,128)(2,1)} copy(bf16[1,2048,1024]{2,1,0:T(8,128)(2,1)} %param.15) | data formatting | bytes 8388608 | tf_op args[4]
  53.0 19.0 %collective-permute-done = bf16[1,256,2048]{2,1,0:T(8,128)(2,1)} collective-permute-done((bf16[1,256,2048]{2,1,0:T(8,128)(2,1)}, bf16[1,256,2048]{2,1,0:T(8,128)(2,1)}, u32[]{:S(2)}, u32[]{:S(2)}) %collective-permute-start) | collective-permute-done | bytes 1048608 | tf_op jit(solution)/shard_map/ppermute | solution.py:29
  72.0 53.2 %collective-permute-done.1 = bf16[1,256,2048]{2,1,0:T(8,128)(2,1)} collective-permute-done((bf16[1,256,2048]{2,1,0:T(8,128)(2,1)}, bf16[1,256,2048]{2,1,0:T(8,128)(2,1)}, u32[]{:S(2)}, u32[]{:S(2)}) %collective-permute-start.1) | collective-permute-done | bytes 1048608 | tf_op jit(solution)/shard_map/ppermute | solution.py:29
  128.8 5.0 %gather_fusion = bf16[4,256,2048]{2,1,0:T(8,128)(2,1)} fusion(bf16[4,256,2048]{2,1,0:T(8,128)(2,1)} %maximum_bitcast_fusion, s32[1024]{0:T(1024)S(1)} %pad_clamp_fusion.1), kind=kCustom, calls=%fused_computation | custom fusion | bytes 8388624 | tf_op jit(solution)/shard_map/gather | solution.py:30
  133.8 57.0 %while.14 = (s32[]{:T(128)}, f32[2048,1024]{1,0:T(8,128)}, bf16[1024,2048]{1,0:T(8,128)(2,1)}, bf16[1,1024,1024]{2,1,0:T(8,128)(2,1)}, s32[]{:T(128)}, /*index=5*/s32[]{:T(128)}, s32[]{:T(128)}, s32[]{:T(128)}) while((s32[]{:T(128)}, f32[2048,1024]{1,0:T(8,128)}, bf16[1024,2048]{1,0:T(8,128)(2,1)}, ...), condition=%wide.region_1.2_spmd.clone, body=%wide.region_0.1_spmd.clone.sunk | while | flops 1082130432 | bytes 26739852 | solution.py:69
  133.8 4.7 %convolution_convert_fusion.2 = bf16[2048,1024]{1,0:T(8,128)(2,1)} fusion(bf16[1024,2048]{1,0:T(8,128)(2,1)} %get-tuple-element.173, s32[]{:T(128)S(6)} %select_n.99, bf16[1,1024,1024]{2,1,0:T(8,128)(2,1)} %get-tuple-element.174), kind=kOutput, calls=%fused_computation.4.clone.1 | convolution fusion | flops 1075838976 | bytes 5768192 | tf_op jit(solution)/shard_map/while/body/eval_jaxpr/dot_general | solution.py:63
  138.5 7.8 %select_add_fusion.2 = f32[2048,1024]{1,0:T(8,128)} fusion(f32[2048,1024]{1,0:T(8,128)} %get-tuple-element.164, bf16[2048,1024]{1,0:T(8,128)(2,1)} %convolution_convert_fusion.2, pred[]{:T(512)S(6)} %compare.13), kind=kLoop, calls=%fused_computation.3.clone.1 | loop fusion | flops 6291456 | bytes 20971520 | tf_op jit(solution)/shard_map/while/body/eval_jaxpr/add | solution.py:67
  146.3 4.7 %convolution_convert_fusion.2 = bf16[2048,1024]{1,0:T(8,128)(2,1)} fusion(bf16[1024,2048]{1,0:T(8,128)(2,1)} %get-tuple-element.173, s32[]{:T(128)S(6)} %select_n.99, bf16[1,1024,1024]{2,1,0:T(8,128)(2,1)} %get-tuple-element.174), kind=kOutput, calls=%fused_computation.4.clone.1 | convolution fusion | flops 1075838976 | bytes 5768192 | tf_op jit(solution)/shard_map/while/body/eval_jaxpr/dot_general | solution.py:63
  151.0 10.2 %select_add_fusion.2 = f32[2048,1024]{1,0:T(8,128)} fusion(f32[2048,1024]{1,0:T(8,128)} %get-tuple-element.164, bf16[2048,1024]{1,0:T(8,128)(2,1)} %convolution_convert_fusion.2, pred[]{:T(512)S(6)} %compare.13), kind=kLoop, calls=%fused_computation.3.clone.1 | loop fusion | flops 6291456 | bytes 20971520 | tf_op jit(solution)/shard_map/while/body/eval_jaxpr/add | solution.py:67
  161.2 4.7 %convolution_convert_fusion.2 = bf16[2048,1024]{1,0:T(8,128)(2,1)} fusion(bf16[1024,2048]{1,0:T(8,128)(2,1)} %get-tuple-element.173, s32[]{:T(128)S(6)} %select_n.99, bf16[1,1024,1024]{2,1,0:T(8,128)(2,1)} %get-tuple-element.174), kind=kOutput, calls=%fused_computation.4.clone.1 | convolution fusion | flops 1075838976 | bytes 5768192 | tf_op jit(solution)/shard_map/while/body/eval_jaxpr/dot_general | solution.py:63
  165.8 10.2 %select_add_fusion.2 = f32[2048,1024]{1,0:T(8,128)} fusion(f32[2048,1024]{1,0:T(8,128)} %get-tuple-element.164, bf16[2048,1024]{1,0:T(8,128)(2,1)} %convolution_convert_fusion.2, pred[]{:T(512)S(6)} %compare.13), kind=kLoop, calls=%fused_computation.3.clone.1 | loop fusion | flops 6291456 | bytes 20971520 | tf_op jit(solution)/shard_map/while/body/eval_jaxpr/add | solution.py:67
  180.7 10.2 %select_add_fusion.2 = f32[2048,1024]{1,0:T(8,128)} fusion(f32[2048,1024]{1,0:T(8,128)} %get-tuple-element.164, bf16[2048,1024]{1,0:T(8,128)(2,1)} %convolution_convert_fusion.2, pred[]{:T(512)S(6)} %compare.13), kind=kLoop, calls=%fused_computation.3.clone.1 | loop fusion | flops 6291456 | bytes 20971520 | tf_op jit(solution)/shard_map/while/body/eval_jaxpr/add | solution.py:67
  190.9 9.1 %copy.39 = f32[2048,1024]{0,1:T(8,128)} copy(f32[2048,1024]{1,0:T(8,128)} %get-tuple-element.84) | data formatting | bytes 16777216 | tf_op jit(solution)/shard_map/while | solution.py:69
  200.0 15.2 %fusion.9 = (bf16[1,2048,1024]{1,2,0:T(8,128)(2,1)}, f32[2048,1024]{0,1:T(8,128)}, bf16[1,2048,1024]{1,2,0:T(8,128)(2,1)}) fusion(f32[2048,1024]{0,1:T(8,128)} %copy.39, bf16[1,2048,1024]{1,2,0:T(8,128)(2,1)} %copy.40, bf16[1,2048,1024]{1,2,0:T(8,128)(2,1)} %copy.33, f32[1,2048,1024]{1,2,0:T(8,128)} %copy.32), kind=kLoop, calls=%fused_computation.18 | loop fusion | flops 35651584 | bytes 41943040 | tf_op jit(solution)/shard_map/broadcast_in_dim | solution.py:88
  221.8 61.7 %reduce-scatter.2.cloned.1.call-done = bf16[256,512]{0,1:T(8,128)(2,1)} async-done(((bf16[2048,512]{0,1:T(8,128)(2,1)}), bf16[256,512]{0,1:T(8,128)(2,1)}) %reduce-scatter.2.cloned.1.call-update) | async-done | bytes 262160 | tf_op jit(solution)/shard_map/reduce_scatter | solution.py:77
  285.4 9.2 %copy.47 = f32[2048,8,128]{2,0,1:T(8,128)} copy(f32[2048,8,128]{0,2,1:T(8,128)} %bitcast.62) | data formatting | bytes 16777216 | tf_op jit(solution)/shard_map/reshape | solution.py:74
  294.6 6.4 %copy.50 = bf16[1,2048,1024]{2,1,0:T(8,128)(2,1)} copy(bf16[1,2048,1024]{1,2,0:T(8,128)(2,1)} %get-tuple-element.124) | data formatting | bytes 8388608
  301.0 6.3 %copy.51 = bf16[1,2048,1024]{2,1,0:T(8,128)(2,1)} copy(bf16[1,2048,1024]{1,2,0:T(8,128)(2,1)} %get-tuple-element.122) | data formatting | bytes 8388608
  317.7 8.0 %scatter_fusion = f32[2048,8,128]{2,0,1:T(8,128)} fusion(f32[2048,8,128]{2,0,1:T(8,128)} %copy.47, s32[4]{0:T(128)S(1)} %get-tuple-element.121, f32[4,2048,128]{2,1,0:T(8,128)} %bitcast.66), kind=kCustom, calls=%fused_computation.2 | custom fusion | bytes 12582928 | tf_op jit(solution)/shard_map/scatter | solution.py:84
  325.8 9.1 %copy.48 = f32[2048,8,128]{0,2,1:T(8,128)} copy(f32[2048,8,128]{2,0,1:T(8,128)} %scatter_fusion) | data formatting | bytes 16777216 | tf_op jit(solution)/shard_map/scatter | solution.py:84
  334.9 9.2 %copy.49 = f32[1,2048,1024]{2,1,0:T(8,128)} copy(f32[1,2048,1024]{1,2,0:T(8,128)} %bitcast.63) | data formatting | bytes 16777216
  (39 shorter events, 43.6 us)
Async XLA Ops:
  7.2 126.7 %all-gather.3.cloned.1.call-start = ((), (), s32[]{:S(2)}) async-start(), calls=%async_computation.1 | async-start | bytes 2621440 | tf_op jit(solution)/shard_map/all_gather | solution.py:57
  7.9 275.6 %reduce-scatter.2.cloned.1.call-start = ((), (), s32[]{:S(2)}) async-start(), calls=%async_computation.2 | async-start | bytes 2359296 | tf_op jit(solution)/shard_map/reduce_scatter | solution.py:77
  20.1 51.9 %collective-permute-start = (bf16[1,256,2048]{2,1,0:T(8,128)(2,1)}, bf16[1,256,2048]{2,1,0:T(8,128)(2,1)}, u32[]{:S(2)}, u32[]{:S(2)}) collective-permute-start(bf16[1,256,2048]{2,1,0:T(8,128)(2,1)} %bitcast.69), channel_id=1, source_target_pairs={{0,1},{1,2},{2,3},{3,0},{4,5},{5,6},{6,7},{7,4},{8,9},{9,10},{10,1... | collective-permute-start | bytes 3145736 | tf_op jit(solution)/shard_map/ppermute | solution.py:29
  24.6 100.6 %collective-permute-start.1 = (bf16[1,256,2048]{2,1,0:T(8,128)(2,1)}, bf16[1,256,2048]{2,1,0:T(8,128)(2,1)}, u32[]{:S(2)}, u32[]{:S(2)}) collective-permute-start(bf16[1,256,2048]{2,1,0:T(8,128)(2,1)} %bitcast.70), channel_id=1, source_target_pairs={{0,2},{1,3},{2,0},{3,1},{4,6},{5,7},{6,4},{7,5},{8,10},{9,11},{10,... | collective-permute-start | bytes 3145736 | tf_op jit(solution)/shard_map/ppermute | solution.py:29
  27.8 97.4 %collective-permute-start.2 = (bf16[1,256,2048]{2,1,0:T(8,128)(2,1)S(1)}, bf16[1,256,2048]{2,1,0:T(8,128)(2,1)}, u32[]{:S(2)}, u32[]{:S(2)}) collective-permute-start(bf16[1,256,2048]{2,1,0:T(8,128)(2,1)S(1)} %bitcast.71), channel_id=1, source_target_pairs={{0,3},{1,0},{2,1},{3,2},{4,7},{5,4},{6,5},{7,6},{8,11},{9,8},{10,9... | collective-permute-start | bytes 3145736 | tf_op jit(solution)/shard_map/ppermute | solution.py:29
  45.6 7.2 %copy-start.2 = (s32[8]{0:T(128)S(1)}, s32[8]{0:T(128)}, u32[]{:S(2)}) copy-start(s32[8]{0:T(128)} %param.18) | copy-start | bytes 100
  219.3 2.0 copy-start
  219.4 2.2 copy-start.1
  221.1 92.5 %all-gather.5.cloned.1.call-start = ((), (), s32[]{:S(2)}) async-start(), calls=%async_computation.3 | async-start | bytes 2359296 | tf_op jit(solution)/shard_map/all_gather | solution.py:81
Sparse Core Ops, SparseCore 0:
  9.5 108.5 all-gather.2
  221.3 62.2 reduce-scatter.1
  285.5 28.0 all-gather.4
